TPU v7x, 32 devices: a whole 2x2x4 slice. The times are simulated.
32 devices in a mesh: dp: 8 (over z, y), mp: 4 (over x, core).
Axes of the slice: x: 2, y: 2, z: 4, core: 2. Of those that a mesh axis runs over, the one named last changes fastest.
Arguments:
- tokens: bfloat16 [192, 196, 768], P('dp'), may hold values from -6 to 6
- cotangent: bfloat16 [192, 196, 768], P('dp'), may hold values from -6 to 6
- counts: int32 [8], replicated, may hold values from 1 to 24, as said below
- vec_params: float32 [5, 768], replicated, as said below
- vec_moments: float32 [2, 5, 768], replicated, as said below
- token_w1: float32 [196, 384], replicated, may hold values from -0.4375 to 0.4375
- token_w1_moments: float32 [2, 196, 384], replicated, as said below
- token_w2: float32 [384, 196], replicated, may hold values from -0.3125 to 0.3125
- token_w2_moments: float32 [2, 384, 196], replicated, as said below
- token_bias: float32 [580], replicated, may hold values from -0.5 to 0.5
- token_bias_moments: float32 [2, 580], replicated, as said below
- chan_w1: float32 [768, 3072], P(None, 'mp'), may hold values from -0.21875 to 0.21875
- chan_w1_moments: float32 [2, 768, 3072], P(None, None, 'mp'), as said below
- chan_b1: float32 [3072], P('mp'), may hold values from -0.5 to 0.5
- chan_b1_moments: float32 [2, 3072], P(None, 'mp'), as said below
- chan_w2: float32 [3072, 768], P('mp'), may hold values from -0.109375 to 0.109375
- chan_w2_moments: float32 [2, 3072, 768], P(None, 'mp'), as said below
Outputs:
- output: bfloat16 [192, 196, 768], P('dp')
- input_grad: bfloat16 [192, 196, 768], P('dp')
- vec_moments_new: float32 [2, 5, 768], replicated
- token_w1_new: float32 [196, 384], replicated
- token_w1_moments_new: float32 [2, 196, 384], replicated
- token_w2_new: float32 [384, 196], replicated
- token_w2_moments_new: float32 [2, 384, 196], replicated
- token_bias_new: float32 [580], replicated
- token_bias_moments_new: float32 [2, 580], replicated
- chan_w1_new: float32 [768, 3072], P(None, 'mp')
- chan_w1_moments_new: float32 [2, 768, 3072], P(None, None, 'mp')
- chan_b1_new: float32 [3072], P('mp')
- chan_b1_moments_new: float32 [2, 3072], P(None, 'mp')
- chan_w2_new: float32 [3072, 768], P('mp')
- chan_w2_moments_new: float32 [2, 3072, 768], P(None, 'mp')
Inputs may be any that keep to these rules, and one draw needn't show every extreme that they name: `counts`: each index of dp holds 1 to 24 live images, the first ones of its slots; some index holds 24. `vec_params`: rows 0 and 2 lie between 0.5 and 1.5. `chan_w1_moments`: the second moments (index 1) are positive. `chan_w2_moments`: the second moments (index 1) are positive. `chan_b1_moments`: the second moments (index 1) are positive. `token_w1_moments`: the second moments (index 1) are positive. `token_w2_moments`: the second moments (index 1) are positive. `token_bias_moments`: the second moments (index 1) are positive. `vec_moments`: the second moments (index 1) are positive.
All inputs are finite; a program needn't handle non-finite values.
Results may differ from a plain program's by a relative error of at most 0.012.
Values may be sent and summed in bfloat16 or wider, within the bound.
No kernel may reach another device: no remote copies, remote signals or barrier semaphores. Data moves between devices by JAX's collectives and lax.ppermute only.
A program may use at most 320 MiB of HBM per device.

v0:
```python
import jax
import jax.numpy as jnp
from jax import lax
from jax.sharding import PartitionSpec as P

STEP = 4
norm_eps = 1e-06
learn_rate = 0.02
decay_rate = 0.5
weight_decay = 0.05
adam_eps = 1e-08


def gelu_exact(values):
    return jax.nn.gelu(values, approximate=False)


def gelu_back(values, grads):
    return jax.vjp(gelu_exact, values)[1](grads)[0]


def norm_parts(values):
    center = values - jnp.mean(values, axis=-1, keepdims=True)
    inv_std = lax.rsqrt(jnp.mean(center * center, axis=-1, keepdims=True) + norm_eps)
    return (center * inv_std, inv_std)


def norm_back(grad_norm, normal, inv_std, gain):
    scaled = grad_norm * gain
    grad_values = inv_std * (
        scaled
        - jnp.mean(scaled, axis=-1, keepdims=True)
        - normal * jnp.mean(scaled * normal, axis=-1, keepdims=True)
    )
    return (grad_values, jnp.sum(grad_norm * normal, axis=(0, 1)), jnp.sum(grad_norm, axis=(0, 1)))


def token_back(token_grad, normed, token_act, token_pre, token_w1_low, token_w2_low):
    token_w2_grad = jnp.einsum(
        "bck,bsc->ks", token_act, token_grad, preferred_element_type=jnp.float32
    )
    out_shift = jnp.sum(token_grad.astype(jnp.float32), axis=(0, 2))
    act_grad = jnp.einsum(
        "bsc,ks->bck", token_grad, token_w2_low, preferred_element_type=jnp.float32
    )
    pre_grad = gelu_back(token_pre, act_grad).astype(jnp.bfloat16)
    token_w1_grad = jnp.einsum("bsc,bck->sk", normed, pre_grad, preferred_element_type=jnp.float32)
    in_shift = jnp.sum(pre_grad.astype(jnp.float32), axis=(0, 1))
    normed_grad = jnp.einsum(
        "bck,sk->bsc", pre_grad, token_w1_low, preferred_element_type=jnp.float32
    )
    return (normed_grad, token_w1_grad, token_w2_grad, jnp.concatenate([in_shift, out_shift]))


def adam_update(weight, moments, grads):
    first = decay_rate * moments[0] + (1.0 - decay_rate) * grads
    second = decay_rate * moments[1] + (1.0 - decay_rate) * grads * grads
    correct = 1.0 - decay_rate**STEP
    step_size = first / correct / (jnp.sqrt(second / correct) + adam_eps)
    return (weight - learn_rate * (step_size + weight_decay * weight), jnp.stack([first, second]))


def new_moments(moments, grads):
    first = decay_rate * moments[0] + (1.0 - decay_rate) * grads
    second = decay_rate * moments[1] + (1.0 - decay_rate) * grads * grads
    return jnp.stack([first, second])


def shards(
    tokens,
    cotangent,
    counts,
    vec_params,
    vec_moments,
    token_w1,
    token_w1_moments,
    token_w2,
    token_w2_moments,
    token_bias,
    token_bias_moments,
    chan_w1,
    chan_w1_moments,
    chan_b1,
    chan_b1_moments,
    chan_w2,
    chan_w2_moments,
):
    images = tokens.shape[0]
    hidden = token_w1.shape[1]
    group_index = lax.axis_index("dp")
    live_count = jnp.sum(jnp.where(jnp.arange(counts.shape[0]) == group_index, counts, 0))
    total = jnp.sum(counts).astype(jnp.float32)
    weight_rows = jnp.where(jnp.arange(images) < live_count, 1.0, 0.0).astype(jnp.float32) / total
    token_w1_low = token_w1.astype(jnp.bfloat16)
    token_w2_low = token_w2.astype(jnp.bfloat16)
    chan_w1_low = chan_w1.astype(jnp.bfloat16)
    chan_w2_low = chan_w2.astype(jnp.bfloat16)
    inputs = tokens.astype(jnp.float32)
    first_norm, first_std = norm_parts(inputs)
    normed = (first_norm * vec_params[0] + vec_params[1]).astype(jnp.bfloat16)
    token_pre = (
        jnp.einsum("bsc,sk->bck", normed, token_w1_low, preferred_element_type=jnp.float32)
        + token_bias[:hidden]
    )
    token_act = gelu_exact(token_pre).astype(jnp.bfloat16)
    token_out = (
        jnp.einsum("bck,ks->bsc", token_act, token_w2_low, preferred_element_type=jnp.float32)
        + token_bias[hidden:][:, None]
    )
    mixed = inputs + token_out
    second_norm, second_std = norm_parts(mixed)
    second = (second_norm * vec_params[2] + vec_params[3]).astype(jnp.bfloat16)
    chan_pre = (
        jnp.einsum("bsc,ch->bsh", second, chan_w1_low, preferred_element_type=jnp.float32) + chan_b1
    )
    chan_act = gelu_exact(chan_pre).astype(jnp.bfloat16)
    partial_out = jnp.einsum(
        "bsh,hc->bsc", chan_act, chan_w2_low, preferred_element_type=jnp.float32
    ).astype(jnp.bfloat16)
    summed = lax.psum(partial_out, "mp").astype(jnp.float32)
    output = (mixed + summed + vec_params[4]).astype(jnp.bfloat16)
    grad_out = cotangent.astype(jnp.float32) * weight_rows[:, None, None]
    grad_low = grad_out.astype(jnp.bfloat16)
    chan_w2_grad = jnp.einsum("bsh,bsc->hc", chan_act, grad_low, preferred_element_type=jnp.float32)
    act_grad = jnp.einsum("bsc,hc->bsh", grad_low, chan_w2_low, preferred_element_type=jnp.float32)
    pre_grad = gelu_back(chan_pre, act_grad).astype(jnp.bfloat16)
    chan_w1_grad = jnp.einsum("bsc,bsh->ch", second, pre_grad, preferred_element_type=jnp.float32)
    chan_b1_grad = jnp.sum(pre_grad.astype(jnp.float32), axis=(0, 1))
    chan_w1_sum, chan_b1_sum, chan_w2_sum = lax.psum(
        (chan_w1_grad, chan_b1_grad, chan_w2_grad), "dp"
    )
    second_part = jnp.einsum(
        "bsh,ch->bsc", pre_grad, chan_w1_low, preferred_element_type=jnp.float32
    )
    second_grad = lax.psum(second_part.astype(jnp.bfloat16), "mp").astype(jnp.float32)
    core_two, gain_two, shift_two = norm_back(second_grad, second_norm, second_std, vec_params[2])
    mixed_grad = grad_out + core_two
    out_shift = jnp.sum(grad_low.astype(jnp.float32), axis=(0, 1))
    token_grad = mixed_grad.astype(jnp.bfloat16)
    normed_grad, token_w1_grad, token_w2_grad, token_bias_grad = token_back(
        token_grad, normed, token_act, token_pre, token_w1_low, token_w2_low
    )
    core_one, gain_one, shift_one = norm_back(normed_grad, first_norm, first_std, vec_params[0])
    input_grad = (mixed_grad + core_one).astype(jnp.bfloat16)
    vec_grad = jnp.stack([gain_one, shift_one, gain_two, shift_two, out_shift])
    vec_sum, token_w1_sum, token_w2_sum, token_bias_sum = lax.psum(
        (vec_grad, token_w1_grad, token_w2_grad, token_bias_grad), "dp"
    )
    vec_moments_new = new_moments(vec_moments, vec_sum)
    token_w1_new, token_w1_moments_new = adam_update(token_w1, token_w1_moments, token_w1_sum)
    token_w2_new, token_w2_moments_new = adam_update(token_w2, token_w2_moments, token_w2_sum)
    token_bias_new, token_bias_moments_new = adam_update(
        token_bias, token_bias_moments, token_bias_sum
    )
    chan_w1_new, chan_w1_moments_new = adam_update(chan_w1, chan_w1_moments, chan_w1_sum)
    chan_b1_new, chan_b1_moments_new = adam_update(chan_b1, chan_b1_moments, chan_b1_sum)
    chan_w2_new, chan_w2_moments_new = adam_update(chan_w2, chan_w2_moments, chan_w2_sum)
    return (
        output,
        input_grad,
        vec_moments_new,
        token_w1_new,
        token_w1_moments_new,
        token_w2_new,
        token_w2_moments_new,
        token_bias_new,
        token_bias_moments_new,
        chan_w1_new,
        chan_w1_moments_new,
        chan_b1_new,
        chan_b1_moments_new,
        chan_w2_new,
        chan_w2_moments_new,
    )


def solution(mesh):
    placed = (
        P("dp", None, None),
        P("dp", None, None),
        P(),
        P(),
        P(),
        P(),
        P(),
        P(),
        P(),
        P(),
        P(),
        P(None, "mp"),
        P(None, None, "mp"),
        P("mp"),
        P(None, "mp"),
        P("mp", None),
        P(None, "mp", None),
    )
    return jax.shard_map(
        shards,
        mesh=mesh,
        in_specs=placed,
        out_specs=(
            P("dp", None, None),
            P("dp", None, None),
            P(),
            P(),
            P(),
            P(),
            P(),
            P(),
            P(),
            P(None, "mp"),
            P(None, None, "mp"),
            P("mp"),
            P(None, "mp"),
            P("mp", None),
            P(None, "mp", None),
        ),
        check_vma=False,
    )
```

profile of v0, /device:TPU:0, one launch (start us, length us, event | category | flops | bytes accessed | tf_op | source)
XLA Modules:
  0.0 795.4 jit_solution(14750361064917613112)
XLA Ops:
  17.2 7.0 fusion.23
  24.2 24.1 %convert_reduce_fusion.1 = (u32[768,384]{1,0:T(8,128)S(1)}, u32[768,384]{1,0:T(8,128)S(1)}, f32[24,768,384]{2,1,0:T(8,128)}) fusion(f32[384]{0:T(512)S(1)} %slice.67, f32[196,384]{1,0:T(8,128)} %param.22, f32[768]{0:T(1024)S(1)} %get-tuple-element.58, f32[768]{0:T(1024)S(1)} %get-tuple-element.59, f32[24,196]{1,0:T(8,128)S(1)} %add_rsqrt_fusion.1, ...), kind=kOutput, calls=%fused_computation.6 | convolution fusion | flops 2880628224 | bytes 38242560 | tf_op jit(solution)/shard_map/bsc,sk->bck/dot_general | solution.py:102
  48.4 67.2 %multiply_convert_fusion = (bf16[24,768,384]{2,1,0:T(8,128)(2,1)}, f32[24,768,384]{2,1,0:T(8,128)}) fusion(f32[24,768,384]{2,1,0:T(8,128)} %get-tuple-element.110, f32[384]{0:T(512)S(1)} %slice.67, u32[768,384]{1,0:T(8,128)S(1)} %get-tuple-element.46, u32[768,384]{1,0:T(8,128)S(1)} %get-tuple-element.45), kind=kLoop, calls=%fused_computation.9 | loop fusion | flops 488374272 | bytes 73139712 | tf_op jit(solution)/shard_map/convert_element_type | solution.py:105
  115.6 11.3 %fusion.101 = (f32[24,196]{1,0:T(8,128)S(1)}, f32[24,196,768]{2,1,0:T(8,128)S(1)}) fusion(f32[196]{0:T(256)S(1)} %slice.68, bf16[24,768,384]{2,1,0:T(8,128)(2,1)} %get-tuple-element.86, f32[384,196]{0,1:T(8,128)S(1)} %copy-done.7, bf16[24,196,768]{2,0,1:T(8,128)(2,1)} %param.17), kind=kOutput, calls=%fused_computation.194 | convolution fusion | flops 2789053440 | bytes 36152464 | tf_op jit(solution)/shard_map/bck,ks->bsc/dot_general | solution.py:107
  130.3 13.9 %convert_reduce_fusion.6 = (u32[196,768]{1,0:T(8,128)S(1)}, u32[196,768]{1,0:T(8,128)S(1)}, f32[24,196,768]{2,1,0:T(8,128)}) fusion(f32[768]{0:T(1024)S(1)} %copy-done.18, f32[768,768]{1,0:T(8,128)S(1)} %copy-done.2, f32[24,196,768]{2,1,0:T(8,128)S(1)} %get-tuple-element.112, f32[768]{0:T(1024)S(1)} %get-tuple-element.60, f32[768]{0:T(1024)S(1)} %get-tuple-element.57, ...), kind=kOutput, calls=%fused_computation.57 | convolution fusion | flops 5610768384 | bytes 32511744 | tf_op jit(solution)/shard_map/bsc,ch->bsh/dot_general | solution.py:114
  144.2 36.2 %multiply_convert_fusion.1 = (bf16[24,196,768]{2,1,0:T(8,128)(2,1)S(1)}, f32[24,196,768]{2,1,0:T(8,128)}) fusion(f32[24,196,768]{2,1,0:T(8,128)} %get-tuple-element.113, f32[768]{0:T(1024)S(1)} %copy-done.18, u32[196,768]{1,0:T(8,128)S(1)} %get-tuple-element.53, u32[196,768]{1,0:T(8,128)S(1)} %get-tuple-element.52), kind=kLoop, calls=%fused_computation.66 | loop fusion | flops 249274368 | bytes 37334016 | tf_op jit(solution)/shard_map/convert_element_type | solution.py:116
  180.4 26.0 %convert_reduce_fusion.7 = (f32[768]{0:T(1024)}, bf16[24,196,768]{2,1,0:T(8,128)(2,1)}) fusion(f32[24,196,768]{2,1,0:T(8,128)} %get-tuple-element.85, f32[768,768]{1,0:T(8,128)S(1)} %copy-done.4, f32[24]{0:T(128)S(1)} %fusion.88, bf16[24,196,768]{2,0,1:T(8,128)(2,1)} %param.18, f32[24,196,768]{2,1,0:T(8,128)} %get-tuple-element.113, f32[768]{0:T(1024)S(1)} %copy-done.18), kind=kOutput, calls=%fused_computation.59 | convolution fusion | flops 5621906432 | bytes 45717600 | tf_op jit(solution)/shard_map/bsc,hc->bsh/dot_general | solution.py:125
  206.4 11.2 %convolution_convert_fusion = bf16[24,196,768]{2,1,0:T(8,128)(2,1)} fusion(bf16[24,196,768]{2,1,0:T(8,128)(2,1)} %get-tuple-element.118, f32[768,768]{1,0:T(8,128)S(1)} %copy-done.3), kind=kOutput, calls=%fused_computation.83 | convolution fusion | flops 5553266688 | bytes 16809984 | tf_op jit(solution)/shard_map/bsh,ch->bsc/dot_general | solution.py:132
  217.6 8.0 %convolution_convert_fusion.1 = bf16[24,196,768]{2,1,0:T(8,128)(2,1)} fusion(bf16[24,196,768]{2,1,0:T(8,128)(2,1)S(1)} %get-tuple-element.84, f32[768,768]{1,0:T(8,128)S(1)} %copy-done.4), kind=kOutput, calls=%fused_computation.84 | convolution fusion | flops 5553266688 | bytes 16809984 | tf_op jit(solution)/shard_map/bsh,hc->bsc/dot_general | solution.py:117
  230.7 14.2 %convolution_bitcast_fusion = f32[768,768]{1,0:T(8,128)} fusion(bf16[24,196,768]{2,1,0:T(8,128)(2,1)} %copy-done.1, f32[24]{0:T(128)S(1)} %fusion.88, bf16[24,196,768]{2,0,1:T(8,128)(2,1)} %param.18), kind=kOutput, calls=%fused_computation.99 | convolution fusion | flops 5559902208 | bytes 16810080 | tf_op jit(solution)/shard_map/bsh,bsc->hc/dot_general | solution.py:124
  245.0 12.1 %convolution_bitcast_fusion.1 = f32[768,768]{1,0:T(8,128)} fusion(bf16[24,196,768]{2,1,0:T(8,128)(2,1)} %get-tuple-element.118, f32[24,196,768]{2,1,0:T(8,128)S(1)} %bitcast.144, f32[768]{0:T(1024)S(1)} %get-tuple-element.60, f32[768]{0:T(1024)S(1)} %get-tuple-element.57, f32[24,196]{1,0:T(8,128)S(1)} %add_rsqrt_fusion, ...), kind=kOutput, calls=%fused_computation.100 | convolution fusion | flops 5567127552 | bytes 24079104 | tf_op jit(solution)/shard_map/bsc,bsh->ch/dot_general | solution.py:127
  257.1 227.4 %all-reduce.8.cloned.1.call-done = (bf16[24,196,768]{2,1,0:T(8,128)(2,1)}, bf16[24,196,768]{2,1,0:T(8,128)(2,1)}) async-done(((bf16[24,196,768]{2,1,0:T(8,128)(2,1)}, bf16[24,196,768]{2,1,0:T(8,128)(2,1)}), (bf16[24,196,768]{2,1,0:T(8,128)(2,1)}, bf16[24,196,768]{2,1,0:T(8,128)(2,1)})) %all-reduce.8.cloned.1.call-update) | async-done | bytes 14450704 | tf_op jit(solution)/shard_map/psum | solution.py:120
  484.5 12.4 %fusion.29 = (f32[768]{0:T(1024)S(1)}, f32[24,196]{1,0:T(8,128)S(1)}, f32[24,196]{1,0:T(8,128)S(1)}, f32[768]{0:T(1024)S(1)}) fusion(bf16[24,196,768]{2,1,0:T(8,128)(2,1)} %get-tuple-element.75, f32[24,196,768]{2,1,0:T(8,128)} %copy-done, f32[24,196]{1,0:T(8,128)S(1)} %add_rsqrt_fusion, f32[24,196]{1,0:T(8,128)S(1)} %broadcast_multiply_fusion.4, ...), kind=kLoop, calls=%fused_computation.52 | loop fusion | flops 36115776 | bytes 21760512 | tf_op jit(solution)/shard_map/reduce_sum | solution.py:35
  497.0 24.4 %convert_reduce_fusion.8 = (f32[196]{0:T(256)}, f32[24,196,768]{2,1,0:T(8,128)}, bf16[24,196,768]{2,1,0:T(8,128)(2,1)}, f32[768]{0:T(1024)S(1)}) fusion(f32[24,196]{1,0:T(8,128)S(1)} %get-tuple-element.119, f32[24,196,768]{2,1,0:T(8,128)} %copy-done, f32[24,196]{1,0:T(8,128)S(1)} %broadcast_multiply_fusion.4, f32[24,196]{1,0:T(8,128)S(1)} %get-tuple-element.120, ...), kind=kLoop, calls=%fused_computation.60 | loop fusion | flops 75865152 | bytes 57888112 | tf_op jit(solution)/shard_map/reduce_sum | solution.py:42
  521.4 13.9 %convolution_bitcast_fusion.2 = f32[384,196]{0,1:T(8,128)} fusion(bf16[24,768,384]{2,1,0:T(8,128)(2,1)} %get-tuple-element.86, f32[24,196,768]{2,1,0:T(8,128)} %get-tuple-element.83), kind=kOutput, calls=%fused_computation.102 | convolution fusion | flops 2778144768 | bytes 28907520 | tf_op jit(solution)/shard_map/bck,bsc->ks/dot_general | solution.py:39
  535.4 30.6 %convert_reduce_fusion.2 = (f32[384]{0:T(512)}, bf16[24,768,384]{2,1,0:T(8,128)(2,1)}) fusion(f32[24,768,384]{2,1,0:T(8,128)} %get-tuple-element.87, f32[384,196]{0,1:T(8,128)S(1)} %copy-done.8, f32[24,196,768]{2,1,0:T(8,128)} %get-tuple-element.83, f32[24,768,384]{2,1,0:T(8,128)} %get-tuple-element.110, f32[384]{0:T(512)S(1)} %copy-done.24), kind=kOutput, calls=%fused_computation.7 | convolution fusion | flops 2898543616 | bytes 85533696 | tf_op jit(solution)/shard_map/bsc,ks->bck/dot_general | solution.py:43
  566.0 11.7 %fusion.45 = f32[196,384]{1,0:T(8,128)} fusion(bf16[24,768,384]{2,1,0:T(8,128)(2,1)} %get-tuple-element.116, f32[768]{0:T(1024)S(1)} %copy-done.28, f32[768]{0:T(1024)S(1)} %copy-done.21, f32[24,196]{1,0:T(8,128)S(1)} %copy-done.15, f32[24,196]{1,0:T(8,128)S(1)} %copy-done.13, bf16[24,196,768]{2,0,1:T(8,128)(2,1)} %param.17), kind=kOutput, calls=%fused_computation.101 | convolution fusion | flops 2796208128 | bytes 21725952 | tf_op jit(solution)/shard_map/bsc,bck->sk/dot_general | solution.py:47
  577.7 19.0 %fusion.22 = (f32[768]{0:T(1024)S(1)}, f32[24,196]{1,0:T(8,128)}, f32[24,196]{1,0:T(8,128)}, f32[24,768,196]{1,2,0:T(8,128)}) fusion(f32[24,196]{1,0:T(8,128)S(1)} %copy-done.15, f32[24,196]{1,0:T(8,128)S(1)} %copy-done.13, bf16[24,196,768]{2,0,1:T(8,128)(2,1)} %param.17, f32[768]{0:T(1024)S(1)} %copy-done.21, ...), kind=kOutput, calls=%fused_computation.45 | convolution fusion | flops 2807111424 | bytes 36214272 | tf_op jit(solution)/shard_map/bck,sk->bsc/dot_general | solution.py:49
  599.0 6.2 reduce_sum.173
  607.8 40.4 %all-reduce = (f32[5,768]{1,0:T(8,128)}, f32[580]{0:T(1024)}, f32[768]{0:T(1024)}) all-reduce(f32[5,768]{1,0:T(8,128)S(1)} %stack.86, f32[580]{0:T(1024)} %pad_maximum_fusion.7, f32[768]{0:T(1024)} %get-tuple-element.117), channel_id=1, replica_groups=mesh['dp'=8,'mp'=4] {'dp'}, use_global_device_ids=true, to_apply=%region_17.18 | all-reduce | flops 5188 | bytes 41504 | tf_op jit(solution)/shard_map/psum | solution.py:146
  653.8 16.5 %fusion.21 = bf16[24,196,768]{2,1,0:T(8,128)(2,1)} fusion(f32[24,196,768]{2,1,0:T(8,128)} %get-tuple-element.83, f32[24,768,196]{1,2,0:T(8,128)} %get-tuple-element.114, f32[24,196]{1,0:T(8,128)S(1)} %broadcast_multiply_fusion, f32[24,196]{1,0:T(8,128)S(1)} %broadcast_multiply_fusion.1, f32[768]{0:T(1024)} %copy-done.20, f32[24,196]{1,0:T(8,128)} %copy-done.14, ...), kind=kLoop, calls=%fused_computation.44 | loop fusion | flops 36126720 | bytes 43430400 | tf_op jit(solution)/shard_map/convert_element_type | solution.py:144
  670.3 7.6 copy.54
  683.5 82.9 %all-reduce.6.cloned.1.call-done = (f32[196,384]{1,0:T(8,128)}, f32[384,196]{0,1:T(8,128)}, f32[768,768]{1,0:T(8,128)}, f32[768,768]{1,0:T(8,128)}) async-done(((f32[196,384]{1,0:T(8,128)}, f32[384,196]{0,1:T(8,128)}, f32[768,768]{1,0:T(8,128)}, f32[768,768]{1,0:T(8,128)}), (f32[196,384]{1,0:T(8,128)}, f32[384,196]{0,1:T(8,128)}, f32[768,768]{1,0:T(8,128)}, ...) | async-done | bytes 5320720 | tf_op jit(solution)/shard_map/psum | solution.py:146
  773.3 6.9 fusion.53
  (138 shorter events, 49.0 us)
Async XLA Ops:
  7.2 477.3 %all-reduce.8.cloned.1.call-start = ((), (), s32[]{:S(2)}) async-start(), calls=%async_computation.1 | async-start | bytes 29491200 | tf_op jit(solution)/shard_map/psum | solution.py:120
  8.6 39.8 %copy-start.23 = (f32[384]{0:T(512)}, f32[384]{0:T(512)S(1)}, u32[]{:S(2)}) copy-start(f32[384]{0:T(512)S(1)} %slice.67) | copy-start | bytes 4612
  12.1 36.2 %copy-start.20 = (f32[768]{0:T(1024)}, f32[768]{0:T(1024)S(1)}, u32[]{:S(2)}) copy-start(f32[768]{0:T(1024)S(1)} %get-tuple-element.59) | copy-start | bytes 9220
  12.1 36.2 %copy-start.27 = (f32[768]{0:T(1024)}, f32[768]{0:T(1024)S(1)}, u32[]{:S(2)}) copy-start(f32[768]{0:T(1024)S(1)} %get-tuple-element.58) | copy-start | bytes 9220
  17.2 31.2 %copy-start.12 = (f32[24,196]{1,0:T(8,128)}, f32[24,196]{1,0:T(8,128)S(1)}, u32[]{:S(2)}) copy-start(f32[24,196]{1,0:T(8,128)S(1)} %broadcast_multiply_fusion.5) | copy-start | bytes 56452
  24.2 24.2 %copy-start.14 = (f32[24,196]{1,0:T(8,128)}, f32[24,196]{1,0:T(8,128)S(1)}, u32[]{:S(2)}) copy-start(f32[24,196]{1,0:T(8,128)S(1)} %add_rsqrt_fusion.1) | copy-start | bytes 56452
  48.4 67.2 %copy-start.7 = (f32[384,196]{0,1:T(8,128)S(1)}, f32[384,196]{0,1:T(8,128)}, u32[]{:S(2)}) copy-start(f32[384,196]{0,1:T(8,128)} %param.24) | copy-start | bytes 903172
  126.9 17.3 %copy-start = (f32[24,196,768]{2,1,0:T(8,128)}, f32[24,196,768]{2,1,0:T(8,128)S(1)}, u32[]{:S(2)}) copy-start(f32[24,196,768]{2,1,0:T(8,128)S(1)} %get-tuple-element.112) | copy-start | bytes 43352068
  144.2 36.2 %copy-start.4 = (f32[768,768]{1,0:T(8,128)S(1)}, f32[768,768]{1,0:T(8,128)}, u32[]{:S(2)}) copy-start(f32[768,768]{1,0:T(8,128)} %param.32) | copy-start | bytes 7077892
  180.4 37.2 %copy-start.1 = (bf16[24,196,768]{2,1,0:T(8,128)(2,1)}, bf16[24,196,768]{2,1,0:T(8,128)(2,1)S(1)}, u32[]{:S(2)}) copy-start(bf16[24,196,768]{2,1,0:T(8,128)(2,1)S(1)} %get-tuple-element.84) | copy-start | bytes 21676036
  180.4 26.0 %copy-start.3 = (f32[768,768]{1,0:T(8,128)S(1)}, f32[768,768]{1,0:T(8,128)}, u32[]{:S(2)}) copy-start(f32[768,768]{1,0:T(8,128)} %param.28) | copy-start | bytes 7077892
  225.7 540.8 %all-reduce.6.cloned.1.call-start = ((), (), s32[]{:S(2)}) async-start(), calls=%async_computation | async-start | bytes 10665984 | tf_op jit(solution)/shard_map/psum | solution.py:146
  229.4 15.5 %slice-start = ((s8[14745600]{0:T(1024)(128)(4,1)}), s8[4194304]{0:T(1024)(128)(4,1)S(1)}, s32[]{:S(2)}) async-start(s8[14745600]{0:T(1024)(128)(4,1)} %bitcast.143), calls=%async_computation.2 | async-start | bytes 8388608
  230.7 14.3 %slice-start.2 = ((s8[14745600]{0:T(1024)(128)(4,1)}), s8[4194304]{0:T(1024)(128)(4,1)S(1)}, s32[]{:S(2)}) async-start(s8[14745600]{0:T(1024)(128)(4,1)} %bitcast.143), calls=%async_computation.4 | async-start | bytes 8388608
  230.7 14.3 %slice-start.3 = ((s8[14745600]{0:T(1024)(128)(4,1)}), s8[2162688]{0:T(1024)(128)(4,1)S(1)}, s32[]{:S(2)}) async-start(s8[14745600]{0:T(1024)(128)(4,1)} %bitcast.143), calls=%async_computation.5 | async-start | bytes 4325376
  257.1 239.9 %copy-start.22 = (f32[768]{0:T(1024)S(1)}, f32[768]{0:T(1024)}, u32[]{:S(2)}) copy-start(f32[768]{0:T(1024)} %get-tuple-element.56) | copy-start | bytes 9220
  535.3 30.6 %copy-start.13 = (f32[24,196]{1,0:T(8,128)S(1)}, f32[24,196]{1,0:T(8,128)}, u32[]{:S(2)}) copy-start(f32[24,196]{1,0:T(8,128)} %copy-done.12) | copy-start | bytes 56452
  535.3 30.6 %copy-start.15 = (f32[24,196]{1,0:T(8,128)S(1)}, f32[24,196]{1,0:T(8,128)}, u32[]{:S(2)}) copy-start(f32[24,196]{1,0:T(8,128)} %copy-done.14) | copy-start | bytes 56452
  535.3 30.6 %copy-start.21 = (f32[768]{0:T(1024)S(1)}, f32[768]{0:T(1024)}, u32[]{:S(2)}) copy-start(f32[768]{0:T(1024)} %copy-done.20) | copy-start | bytes 9220
  535.4 30.6 %copy-start.28 = (f32[768]{0:T(1024)S(1)}, f32[768]{0:T(1024)}, u32[]{:S(2)}) copy-start(f32[768]{0:T(1024)} %copy-done.27) | copy-start | bytes 9220
  596.7 51.6 %copy-start.16 = (f32[1,5,768]{2,0,1:T(1,128)S(1)}, f32[1,5,768]{2,0,1:T(1,128)}, u32[]{:S(2)}) copy-start(f32[1,5,768]{2,0,1:T(1,128)} %get-tuple-element.106) | copy-start | bytes 46084
  596.7 54.3 %copy-start.19 = (f32[768]{0:T(1024)S(1)}, f32[768]{0:T(1024)}, u32[]{:S(2)}) copy-start(f32[768]{0:T(1024)} %param.30) | copy-start | bytes 9220
  599.0 78.9 %slice-start.4 = ((s8[7372800]{0:T(1024)(128)(4,1)}), s8[3178496]{0:T(1024)(128)(4,1)S(1)}, s32[]{:S(2)}) async-start(s8[7372800]{0:T(1024)(128)(4,1)} %bitcast.145), calls=%async_computation.6 | async-start | bytes 6356992
  653.8 24.1 %slice-start.5 = ((s8[7372800]{0:T(1024)(128)(4,1)}), s8[4194304]{0:T(1024)(128)(4,1)S(1)}, s32[]{:S(2)}) async-start(s8[7372800]{0:T(1024)(128)(4,1)} %bitcast.145), calls=%async_computation.7 | async-start | bytes 8388608
  (19 other events, 168.7 us)
Sparse Core Ops, SparseCore 0:
  225.8 258.6 all-reduce.7
  577.8 188.6 all-reduce.5
where the time goes:
time: 799 us; the launch traced here: 795 us
  waiting for transfers between devices  310 us (39%)
  other arithmetic  208 us (26%)
  matrix products  196 us (25%)
  blocking collectives  40.4 us (5%)
  local copies, waits for them, and re-layouts  25.7 us (3%)
  between operations  15.3 us (2%)
    psum x1, waiting for transfers between devices, shards(): summed = lax.psum(partial_out, 'mp').astype(jnp.float32)  227 us
    psum x1, waiting for transfers between devices, shards(): lax.psum((vec_grad, token_w1_grad, token_w2_grad, token_bias_grad), 'dp')  82.9 us
    convert_element_type x1, other arithmetic, shards(): token_act = gelu_exact(token_pre).astype(jnp.bfloat16)  67.2 us
    psum x1, blocking collectives, shards(): lax.psum((vec_grad, token_w1_grad, token_w2_grad, token_bias_grad), 'dp')  40.4 us
    convert_element_type x1, other arithmetic, shards(): chan_act = gelu_exact(chan_pre).astype(jnp.bfloat16)  36.2 us
    dot_general x1, matrix products, token_back(): jnp.einsum('bsc,ks->bck', token_grad, token_w2_low, preferred_element_typ...  30.6 us
    dot_general x1, matrix products, shards(): jnp.einsum('bsc,hc->bsh', grad_low, chan_w2_low, preferred_element_type=j...  26 us
    reduce_sum x1, other arithmetic, token_back(): out_shift = jnp.sum(token_grad.astype(jnp.float32), axis=(0, 2))  24.4 us
  transfers between devices with their start and end apart: 2, of which 2 were waited for; matrix products, arithmetic and copies ran while one was open for 12% of the time, Pallas kernels for 0%

commit v1 on v0

--- a/solution.py
+++ b/solution.py
@@ -117,7 +117,7 @@
     partial_out = jnp.einsum(
         "bsh,hc->bsc", chan_act, chan_w2_low, preferred_element_type=jnp.float32
     ).astype(jnp.bfloat16)
-    summed = lax.psum(partial_out, "mp").astype(jnp.float32)
+    summed = jnp.sum(lax.all_gather(partial_out, "mp"), axis=0).astype(jnp.float32)
     output = (mixed + summed + vec_params[4]).astype(jnp.bfloat16)
     grad_out = cotangent.astype(jnp.float32) * weight_rows[:, None, None]
     grad_low = grad_out.astype(jnp.bfloat16)

time: 799 us -> 847 us (1.060)
  waiting for transfers between devices: 310 us -> 345 us
  other arithmetic: 208 us -> 222 us
    all_gather x0 -> x1, waiting for transfers between devices: none -> 165 us  [shards(): lax.all_gather(partial_out, 'mp')]
    psum x1, waiting for transfers between devices: 227 us -> 96.3 us  [shards(): lax.psum(second_part.astype(jnp.bfloat16), 'mp').astype(jnp.float32)]
    reduce_sum x0 -> x1, other arithmetic: none -> 14.5 us  [shards(): jnp.sum(lax.all_gather(partial_out, 'mp'), axis=0).astype(jnp.float32)]
    unnamed x87 -> x79, local copies, waits for them, and re-layouts: 15.9 us -> 18.3 us
  transfers between devices with their start and end apart: 2 -> 3, of which waited for: 2 -> 3; matrix products, arithmetic and copies ran while one was open for 12% -> 14% of each run, Pallas kernels for 0% -> 0%
where the time goes in v1:
time: 847 us; the launch traced here: 844 us
  waiting for transfers between devices  345 us (41%)
  other arithmetic  222 us (26%)
  matrix products  188 us (22%)
  blocking collectives  40.7 us (5%)
  local copies, waits for them, and re-layouts  32.5 us (4%)
  between operations  15 us (2%)
    all_gather x1, waiting for transfers between devices, shards(): lax.all_gather(partial_out, 'mp')  165 us
    psum x1, waiting for transfers between devices, shards(): lax.psum(second_part.astype(jnp.bfloat16), 'mp').astype(jnp.float32)  96.3 us
    psum x1, waiting for transfers between devices, shards(): lax.psum((vec_grad, token_w1_grad, token_w2_grad, token_bias_grad), 'dp')  83.8 us
    convert_element_type x1, other arithmetic, shards(): token_act = gelu_exact(token_pre).astype(jnp.bfloat16)  67.2 us
    psum x1, blocking collectives, shards(): lax.psum((vec_grad, token_w1_grad, token_w2_grad, token_bias_grad), 'dp')  40.7 us
    convert_element_type x1, other arithmetic, shards(): chan_act = gelu_exact(chan_pre).astype(jnp.bfloat16)  36.3 us
    dot_general x1, matrix products, token_back(): jnp.einsum('bsc,ks->bck', token_grad, token_w2_low, preferred_element_typ...  30.6 us
    reduce_sum x1, other arithmetic, token_back(): out_shift = jnp.sum(token_grad.astype(jnp.float32), axis=(0, 2))  24.5 us
  transfers between devices with their start and end apart: 3, of which 3 were waited for; matrix products, arithmetic and copies ran while one was open for 14% of the time, Pallas kernels for 0%

profile of v1, /device:TPU:0, one launch (start us, length us, event | category | flops | bytes accessed | tf_op | source)
XLA Modules:
  0.0 843.9 jit_solution(2870631457323520814)
XLA Ops:
  17.2 7.0 fusion.23
  24.2 23.9 %convert_reduce_fusion.1 = (u32[768,384]{1,0:T(8,128)S(1)}, u32[768,384]{1,0:T(8,128)S(1)}, f32[24,768,384]{2,1,0:T(8,128)}) fusion(f32[384]{0:T(512)S(1)} %slice.67, f32[196,384]{1,0:T(8,128)} %param.22, f32[768]{0:T(1024)S(1)} %get-tuple-element.88, f32[768]{0:T(1024)S(1)} %get-tuple-element.89, f32[24,196]{1,0:T(8,128)S(1)} %add_rsqrt_fusion.1, ...), kind=kOutput, calls=%fused_computation.6 | convolution fusion | flops 2880628224 | bytes 38242560 | tf_op jit(solution)/shard_map/bsc,sk->bck/dot_general | solution.py:102
  48.2 67.2 %multiply_convert_fusion = (bf16[24,768,384]{2,1,0:T(8,128)(2,1)}, f32[24,768,384]{2,1,0:T(8,128)}) fusion(f32[24,768,384]{2,1,0:T(8,128)} %get-tuple-element.138, f32[384]{0:T(512)S(1)} %slice.67, u32[768,384]{1,0:T(8,128)S(1)} %get-tuple-element.76, u32[768,384]{1,0:T(8,128)S(1)} %get-tuple-element.75), kind=kLoop, calls=%fused_computation.9 | loop fusion | flops 488374272 | bytes 73139712 | tf_op jit(solution)/shard_map/convert_element_type | solution.py:105
  115.4 11.3 %fusion.101 = (f32[24,196]{1,0:T(8,128)S(1)}, f32[24,196,768]{2,1,0:T(8,128)S(1)}) fusion(f32[196]{0:T(256)S(1)} %slice.68, bf16[24,768,384]{2,1,0:T(8,128)(2,1)} %get-tuple-element.114, f32[384,196]{0,1:T(8,128)S(1)} %copy-done.6, bf16[24,196,768]{2,0,1:T(8,128)(2,1)} %param.17), kind=kOutput, calls=%fused_computation.194 | convolution fusion | flops 2789053440 | bytes 36152464 | tf_op jit(solution)/shard_map/bck,ks->bsc/dot_general | solution.py:107
  130.2 13.9 %convert_reduce_fusion.6 = (u32[196,768]{1,0:T(8,128)S(1)}, u32[196,768]{1,0:T(8,128)S(1)}, f32[24,196,768]{2,1,0:T(8,128)}) fusion(f32[768]{0:T(1024)S(1)} %copy-done.17, f32[768,768]{1,0:T(8,128)S(1)} %copy-done.1, f32[24,196,768]{2,1,0:T(8,128)S(1)} %get-tuple-element.140, f32[768]{0:T(1024)S(1)} %get-tuple-element.90, f32[768]{0:T(1024)S(1)} %get-tuple-element.87, ...), kind=kOutput, calls=%fused_computation.57 | convolution fusion | flops 5610768384 | bytes 32511744 | tf_op jit(solution)/shard_map/bsc,ch->bsh/dot_general | solution.py:114
  144.1 36.3 %multiply_convert_fusion.1 = (bf16[24,196,768]{2,1,0:T(8,128)(2,1)}, f32[24,196,768]{2,1,0:T(8,128)}) fusion(f32[24,196,768]{2,1,0:T(8,128)} %get-tuple-element.141, f32[768]{0:T(1024)S(1)} %copy-done.17, u32[196,768]{1,0:T(8,128)S(1)} %get-tuple-element.83, u32[196,768]{1,0:T(8,128)S(1)} %get-tuple-element.82), kind=kLoop, calls=%fused_computation.66 | loop fusion | flops 249274368 | bytes 37334016 | tf_op jit(solution)/shard_map/convert_element_type | solution.py:116
  180.4 21.8 %convert_reduce_fusion.7 = (f32[768]{0:T(1024)}, bf16[24,196,768]{2,1,0:T(8,128)(2,1)S(1)}) fusion(f32[24,196,768]{2,1,0:T(8,128)} %get-tuple-element.113, f32[768,768]{1,0:T(8,128)S(1)} %copy-done.3, f32[24]{0:T(128)S(1)} %fusion.88, bf16[24,196,768]{2,0,1:T(8,128)(2,1)} %param.18, f32[24,196,768]{2,1,0:T(8,128)} %get-tuple-element.141, f32[768]{0:T(1024)S(1)} %copy-done.17), kind=kOutput, calls=%fused_computation.59 | convolution fusion | flops 5621906432 | bytes 45717600 | tf_op jit(solution)/shard_map/bsc,hc->bsh/dot_general | solution.py:125
  205.2 8.0 convolution_convert_fusion
  213.3 9.5 %convolution_convert_fusion.1 = bf16[24,196,768]{2,1,0:T(8,128)(2,1)S(1)} fusion(bf16[24,196,768]{2,1,0:T(8,128)(2,1)} %get-tuple-element.112, f32[768,768]{1,0:T(8,128)S(1)} %copy-done.3), kind=kOutput, calls=%fused_computation.84 | convolution fusion | flops 5553266688 | bytes 16809984 | tf_op jit(solution)/shard_map/bsh,hc->bsc/dot_general | solution.py:117
  232.1 12.8 %convolution_bitcast_fusion = f32[768,768]{1,0:T(8,128)} fusion(bf16[24,196,768]{2,1,0:T(8,128)(2,1)} %get-tuple-element.112, f32[24]{0:T(128)S(1)} %fusion.88, bf16[24,196,768]{2,0,1:T(8,128)(2,1)} %param.18), kind=kOutput, calls=%fused_computation.99 | convolution fusion | flops 5559902208 | bytes 16810080 | tf_op jit(solution)/shard_map/bsh,bsc->hc/dot_general | solution.py:124
  244.9 12.1 %convolution_bitcast_fusion.1 = f32[768,768]{1,0:T(8,128)} fusion(bf16[24,196,768]{2,1,0:T(8,128)(2,1)} %copy-done.28, f32[24,196,768]{2,1,0:T(8,128)S(1)} %bitcast.145, f32[768]{0:T(1024)S(1)} %get-tuple-element.90, f32[768]{0:T(1024)S(1)} %get-tuple-element.87, f32[24,196]{1,0:T(8,128)S(1)} %add_rsqrt_fusion, f32[24,196]{1,0:T(8,128)S(1)} %broadcast_multiply_fusion.4), kind=kOutput, calls=%fused_computation.100 | convolution fusion | flops 5567127552 | bytes 24079104 | tf_op jit(solution)/shard_map/bsc,bsh->ch/dot_general | solution.py:127
  257.0 96.3 %all-reduce.5.cloned.1.call-done = bf16[24,196,768]{2,1,0:T(8,128)(2,1)} async-done(((bf16[24,196,768]{2,1,0:T(8,128)(2,1)}), bf16[24,196,768]{2,1,0:T(8,128)(2,1)}) %all-reduce.5.cloned.1.call-update) | async-done | bytes 7225360 | tf_op jit(solution)/shard_map/psum | solution.py:135
  353.3 12.0 %fusion.29 = (f32[768]{0:T(1024)S(1)}, f32[24,196]{1,0:T(8,128)S(1)}, f32[24,196]{1,0:T(8,128)S(1)}, f32[768]{0:T(1024)S(1)}) fusion(bf16[24,196,768]{2,1,0:T(8,128)(2,1)} %all-reduce.5.cloned.1.call-done, f32[24,196,768]{2,1,0:T(8,128)} %copy-done, f32[24,196]{1,0:T(8,128)S(1)} %add_rsqrt_fusion, f32[24,196]{1,0:T(8,128)S(1)} %broadcast_multiply_fusion.4, ...), kind=kLoop, calls=%fused_computation.52 | loop fusion | flops 36115776 | bytes 21760512 | tf_op jit(solution)/shard_map/reduce_sum | solution.py:35
  366.5 164.7 %all-gather.3.cloned.1.call-done = bf16[96,196,768]{2,0,1:T(8,128)(2,1)} async-done(((bf16[24,196,768]{2,0,1:T(8,128)(2,1)}), bf16[96,196,768]{2,0,1:T(8,128)(2,1)}) %all-gather.3.cloned.1.call-update) | async-done | bytes 28901392 | tf_op jit(solution)/shard_map/all_gather | solution.py:120
  531.2 14.5 %reduce_sum.178 = bf16[24,196,768]{2,0,1:T(8,128)(2,1)} reduce(bf16[4,24,196,768]{3,1,0,2:T(8,128)(2,1)} %bitcast.148, bf16[]{:T(256)} %constant.73.clone.1), dimensions={0}, to_apply=%region_4.5 | reduce | flops 10838016 | bytes 36126720 | tf_op jit(solution)/shard_map/reduce_sum | solution.py:120
  545.7 24.5 %convert_reduce_fusion.8 = (f32[196]{0:T(256)}, f32[24,196,768]{2,1,0:T(8,128)}, bf16[24,196,768]{2,1,0:T(8,128)(2,1)}, f32[768]{0:T(1024)S(1)}) fusion(f32[24,196]{1,0:T(8,128)S(1)} %get-tuple-element.147, f32[24,196,768]{2,1,0:T(8,128)} %copy-done, f32[24,196]{1,0:T(8,128)S(1)} %broadcast_multiply_fusion.4, f32[24,196]{1,0:T(8,128)S(1)} %get-tuple-element.148, ...), kind=kLoop, calls=%fused_computation.60 | loop fusion | flops 75865152 | bytes 57888112 | tf_op jit(solution)/shard_map/reduce_sum | solution.py:42
  570.2 13.9 %convolution_bitcast_fusion.2 = f32[384,196]{0,1:T(8,128)} fusion(bf16[24,768,384]{2,1,0:T(8,128)(2,1)} %get-tuple-element.114, f32[24,196,768]{2,1,0:T(8,128)} %get-tuple-element.111), kind=kOutput, calls=%fused_computation.102 | convolution fusion | flops 2778144768 | bytes 28907520 | tf_op jit(solution)/shard_map/bck,bsc->ks/dot_general | solution.py:39
  584.2 30.6 %convert_reduce_fusion.2 = (f32[384]{0:T(512)}, bf16[24,768,384]{2,1,0:T(8,128)(2,1)}) fusion(f32[24,768,384]{2,1,0:T(8,128)} %get-tuple-element.115, f32[384,196]{0,1:T(8,128)S(1)} %copy-done.7, f32[24,196,768]{2,1,0:T(8,128)} %get-tuple-element.111, f32[24,768,384]{2,1,0:T(8,128)} %get-tuple-element.138, f32[384]{0:T(512)S(1)} %copy-done.23), kind=kOutput, calls=%fused_computation.7 | convolution fusion | flops 2898543616 | bytes 85533696 | tf_op jit(solution)/shard_map/bsc,ks->bck/dot_general | solution.py:43
  614.9 11.7 %fusion.45 = f32[196,384]{1,0:T(8,128)} fusion(bf16[24,768,384]{2,1,0:T(8,128)(2,1)} %get-tuple-element.144, f32[768]{0:T(1024)S(1)} %copy-done.27, f32[768]{0:T(1024)S(1)} %copy-done.21, f32[24,196]{1,0:T(8,128)S(1)} %copy-done.14, f32[24,196]{1,0:T(8,128)S(1)} %copy-done.12, bf16[24,196,768]{2,0,1:T(8,128)(2,1)} %param.17), kind=kOutput, calls=%fused_computation.101 | convolution fusion | flops 2796208128 | bytes 21725952 | tf_op jit(solution)/shard_map/bsc,bck->sk/dot_general | solution.py:47
  626.7 18.8 %fusion.22 = (f32[768]{0:T(1024)S(1)}, f32[24,196]{1,0:T(8,128)}, f32[24,196]{1,0:T(8,128)}, f32[24,768,196]{1,2,0:T(8,128)}) fusion(f32[24,196]{1,0:T(8,128)S(1)} %copy-done.14, f32[24,196]{1,0:T(8,128)S(1)} %copy-done.12, bf16[24,196,768]{2,0,1:T(8,128)(2,1)} %param.17, f32[768]{0:T(1024)S(1)} %copy-done.21, ...), kind=kOutput, calls=%fused_computation.45 | convolution fusion | flops 2807111424 | bytes 36214272 | tf_op jit(solution)/shard_map/bck,sk->bsc/dot_general | solution.py:49
  655.4 40.7 %all-reduce = (f32[5,768]{1,0:T(8,128)}, f32[580]{0:T(1024)}, f32[768]{0:T(1024)}) all-reduce(f32[5,768]{1,0:T(8,128)S(1)} %stack.86, f32[580]{0:T(1024)} %pad_maximum_fusion.7, f32[768]{0:T(1024)} %get-tuple-element.145), channel_id=1, replica_groups=mesh['dp'=8,'mp'=4] {'dp'}, use_global_device_ids=true, to_apply=%region_17.18 | all-reduce | flops 5188 | bytes 41504 | tf_op jit(solution)/shard_map/psum | solution.py:146
  701.6 16.6 %fusion.21 = bf16[24,196,768]{2,1,0:T(8,128)(2,1)} fusion(f32[24,196,768]{2,1,0:T(8,128)} %get-tuple-element.111, f32[24,768,196]{1,2,0:T(8,128)} %get-tuple-element.142, f32[24,196]{1,0:T(8,128)S(1)} %broadcast_multiply_fusion, f32[24,196]{1,0:T(8,128)S(1)} %broadcast_multiply_fusion.1, f32[768]{0:T(1024)} %copy-done.20, f32[24,196]{1,0:T(8,128)} %copy-done.13, ...), kind=kLoop, calls=%fused_computation.44 | loop fusion | flops 36126720 | bytes 43430400 | tf_op jit(solution)/shard_map/convert_element_type | solution.py:144
  718.3 7.6 copy.83
  731.5 83.8 %all-reduce.7.cloned.1.call-done = (f32[196,384]{1,0:T(8,128)}, f32[384,196]{0,1:T(8,128)}, f32[768,768]{1,0:T(8,128)}, f32[768,768]{1,0:T(8,128)}) async-done(((f32[196,384]{1,0:T(8,128)}, f32[384,196]{0,1:T(8,128)}, f32[768,768]{1,0:T(8,128)}, f32[768,768]{1,0:T(8,128)}), (f32[196,384]{1,0:T(8,128)}, f32[384,196]{0,1:T(8,128)}, f32[768,768]{1,0:T(8,128)}, ...) | async-done | bytes 5320720 | tf_op jit(solution)/shard_map/psum | solution.py:146
  (133 shorter events, 69.2 us)
Async XLA Ops:
  7.2 346.1 %all-reduce.5.cloned.1.call-start = ((), (), s32[]{:S(2)}) async-start(), calls=%async_computation | async-start | bytes 14745600 | tf_op jit(solution)/shard_map/psum | solution.py:135
  8.6 39.6 %copy-start.22 = (f32[384]{0:T(512)}, f32[384]{0:T(512)S(1)}, u32[]{:S(2)}) copy-start(f32[384]{0:T(512)S(1)} %slice.67) | copy-start | bytes 4612
  12.1 36.0 %copy-start.20 = (f32[768]{0:T(1024)}, f32[768]{0:T(1024)S(1)}, u32[]{:S(2)}) copy-start(f32[768]{0:T(1024)S(1)} %get-tuple-element.89) | copy-start | bytes 9220
  12.1 36.0 %copy-start.26 = (f32[768]{0:T(1024)}, f32[768]{0:T(1024)S(1)}, u32[]{:S(2)}) copy-start(f32[768]{0:T(1024)S(1)} %get-tuple-element.88) | copy-start | bytes 9220
  17.2 31.0 %copy-start.11 = (f32[24,196]{1,0:T(8,128)}, f32[24,196]{1,0:T(8,128)S(1)}, u32[]{:S(2)}) copy-start(f32[24,196]{1,0:T(8,128)S(1)} %broadcast_multiply_fusion.5) | copy-start | bytes 56452
  24.2 24.0 %copy-start.13 = (f32[24,196]{1,0:T(8,128)}, f32[24,196]{1,0:T(8,128)S(1)}, u32[]{:S(2)}) copy-start(f32[24,196]{1,0:T(8,128)S(1)} %add_rsqrt_fusion.1) | copy-start | bytes 56452
  48.2 67.2 %copy-start.6 = (f32[384,196]{0,1:T(8,128)S(1)}, f32[384,196]{0,1:T(8,128)}, u32[]{:S(2)}) copy-start(f32[384,196]{0,1:T(8,128)} %param.24) | copy-start | bytes 903172
  126.7 17.3 %copy-start = (f32[24,196,768]{2,1,0:T(8,128)}, f32[24,196,768]{2,1,0:T(8,128)S(1)}, u32[]{:S(2)}) copy-start(f32[24,196,768]{2,1,0:T(8,128)S(1)} %get-tuple-element.140) | copy-start | bytes 43352068
  144.1 36.3 %copy-start.3 = (f32[768,768]{1,0:T(8,128)S(1)}, f32[768,768]{1,0:T(8,128)}, u32[]{:S(2)}) copy-start(f32[768,768]{1,0:T(8,128)} %param.32) | copy-start | bytes 7077892
  180.4 24.8 %copy-start.2 = (f32[768,768]{1,0:T(8,128)S(1)}, f32[768,768]{1,0:T(8,128)}, u32[]{:S(2)}) copy-start(f32[768,768]{1,0:T(8,128)} %param.28) | copy-start | bytes 7077892
  213.3 317.9 %all-gather.3.cloned.1.call-start = ((), (), s32[]{:S(2)}) async-start(), calls=%async_computation.1 | async-start | bytes 36126720 | tf_op jit(solution)/shard_map/all_gather | solution.py:120
  227.4 587.9 %all-reduce.7.cloned.1.call-start = ((), (), s32[]{:S(2)}) async-start(), calls=%async_computation.2 | async-start | bytes 10665984 | tf_op jit(solution)/shard_map/psum | solution.py:146
  230.8 14.0 %slice-start = ((s8[14745600]{0:T(1024)(128)(4,1)}), s8[4194304]{0:T(1024)(128)(4,1)S(1)}, s32[]{:S(2)}) async-start(s8[14745600]{0:T(1024)(128)(4,1)} %bitcast.144), calls=%async_computation.3 | async-start | bytes 8388608
  531.2 14.5 %copy-start.19 = (f32[768]{0:T(1024)S(1)}, f32[768]{0:T(1024)}, u32[]{:S(2)}) copy-start(f32[768]{0:T(1024)} %get-tuple-element.86) | copy-start | bytes 9220
  570.2 13.9 %copy-start.7 = (f32[384,196]{0,1:T(8,128)S(1)}, f32[384,196]{0,1:T(8,128)}, u32[]{:S(2)}) copy-start(f32[384,196]{0,1:T(8,128)} %param.24) | copy-start | bytes 903172
  570.2 13.9 %copy-start.23 = (f32[384]{0:T(512)S(1)}, f32[384]{0:T(512)}, u32[]{:S(2)}) copy-start(f32[384]{0:T(512)} %copy-done.22) | copy-start | bytes 4612
  584.2 30.7 %copy-start.12 = (f32[24,196]{1,0:T(8,128)S(1)}, f32[24,196]{1,0:T(8,128)}, u32[]{:S(2)}) copy-start(f32[24,196]{1,0:T(8,128)} %copy-done.11) | copy-start | bytes 56452
  584.2 30.7 %copy-start.14 = (f32[24,196]{1,0:T(8,128)S(1)}, f32[24,196]{1,0:T(8,128)}, u32[]{:S(2)}) copy-start(f32[24,196]{1,0:T(8,128)} %copy-done.13) | copy-start | bytes 56452
  584.2 30.7 %copy-start.21 = (f32[768]{0:T(1024)S(1)}, f32[768]{0:T(1024)}, u32[]{:S(2)}) copy-start(f32[768]{0:T(1024)} %copy-done.20) | copy-start | bytes 9220
  584.2 30.7 %copy-start.27 = (f32[768]{0:T(1024)S(1)}, f32[768]{0:T(1024)}, u32[]{:S(2)}) copy-start(f32[768]{0:T(1024)} %copy-done.26) | copy-start | bytes 9220
  645.4 50.6 %copy-start.15 = (f32[1,5,768]{2,0,1:T(1,128)S(1)}, f32[1,5,768]{2,0,1:T(1,128)}, u32[]{:S(2)}) copy-start(f32[1,5,768]{2,0,1:T(1,128)} %get-tuple-element.134) | copy-start | bytes 46084
  645.4 53.4 %copy-start.18 = (f32[768]{0:T(1024)S(1)}, f32[768]{0:T(1024)}, u32[]{:S(2)}) copy-start(f32[768]{0:T(1024)} %param.30) | copy-start | bytes 9220
  646.6 79.2 %slice-start.4 = ((s8[7372800]{0:T(1024)(128)(4,1)}), s8[3178496]{0:T(1024)(128)(4,1)S(1)}, s32[]{:S(2)}) async-start(s8[7372800]{0:T(1024)(128)(4,1)} %bitcast.146), calls=%async_computation.7 | async-start | bytes 6356992
  701.6 24.2 %slice-start.5 = ((s8[7372800]{0:T(1024)(128)(4,1)}), s8[4194304]{0:T(1024)(128)(4,1)S(1)}, s32[]{:S(2)}) async-start(s8[7372800]{0:T(1024)(128)(4,1)} %bitcast.146), calls=%async_computation.8 | async-start | bytes 8388608
  (16 other events, 138.6 us)
Sparse Core Ops, SparseCore 0:
  213.4 139.8 all-reduce.4
  355.4 175.6 all-gather.2
  626.8 188.4 all-reduce.6
